TPU v7x, 512 devices: a whole 4x8x8 slice. The times are simulated.
512 devices in a mesh: dp: 4 (over x), expert: 128 (over z, y, core).
Axes of the slice: x: 4, y: 8, z: 8, core: 2. Of those that a mesh axis runs over, the one named last changes fastest.
Arguments:
- tokens: bfloat16 [2048, 2048], P('expert', 'dp'), may hold values from -6 to 6
- cotangent: bfloat16 [2048, 2048], P('expert', 'dp'), may hold values from -6 to 6
- expert_ids: int32 [2048, 8], P('expert'), may hold values from 0 to 127, all different within a row; in each aligned block of 16 rows (0 to 15, 16 to 31, ...) at most 2 rows name the same one
- gate_probs: float32 [2048, 8], P('expert'), may hold values from 0.05 to 1
- w_gate: bfloat16 [128, 768, 2048], P('expert', None, 'dp'), may hold values from -0.125 to 0.125
- w_up: bfloat16 [128, 768, 2048], P('expert', None, 'dp'), may hold values from -0.125 to 0.125
- w_down: bfloat16 [128, 768, 2048], P('expert', None, 'dp'), may hold values from -0.21875 to 0.21875
Outputs:
- mixed: bfloat16 [2048, 2048], P('expert', 'dp')
- grad_tokens: bfloat16 [2048, 2048], P('expert', 'dp')
- grad_gate: bfloat16 [128, 768, 2048], P('expert', None, 'dp')
- grad_up: bfloat16 [128, 768, 2048], P('expert', None, 'dp')
- grad_down: bfloat16 [128, 768, 2048], P('expert', None, 'dp')
Inputs may be any that keep to these rules, and one draw needn't show every extreme that they name: `expert_ids`: each token names 8 different experts. The 16 tokens of one index of expert (rows b * 16 to (b + 1) * 16 - 1) name no expert more than 2 times, a bound that some block reaches.
All inputs are finite; a program needn't handle non-finite values.
Results may differ from a plain program's by a relative error of at most 0.02.
Values may be sent and summed in bfloat16 or wider, within the bound.
A program may use at most 64 MiB of HBM per device.

v0:
```python
import jax
import jax.numpy as jnp
from jax import lax
from jax.sharding import PartitionSpec as P


def activate(pre_gate, pre_up, back_hidden):
    sigmas = jax.nn.sigmoid(pre_gate)
    silu_vals = pre_gate * sigmas
    hidden = (silu_vals * pre_up).astype(jnp.bfloat16)
    back_gate = (back_hidden * pre_up * sigmas * (1.0 + pre_gate * (1.0 - sigmas))).astype(
        jnp.bfloat16
    )
    back_up = (back_hidden * silu_vals).astype(jnp.bfloat16)
    return (hidden, back_gate, back_up)


def deliver(outbound):
    return lax.all_to_all(outbound, "expert", split_axis=0, concat_axis=0, tiled=True)


def on_device(tokens, cotangent, expert_ids, gate_probs, w_gate, w_up, w_down):
    tok_rows, columns = tokens.shape
    top_count = expert_ids.shape[1]
    experts = lax.axis_size("expert")
    capacity = min(tok_rows, max(2, 2 * tok_rows * top_count // experts))
    slot_count = experts * capacity
    flat_ids = expert_ids.reshape(-1)
    onehot = (flat_ids[:, None] == jnp.arange(experts, dtype=jnp.int32)[None, :]).astype(jnp.int32)
    before = jnp.cumsum(onehot, axis=0) - onehot
    ranks = jnp.sum(before * onehot, axis=1)
    slot_ids = flat_ids * capacity + ranks
    chosen = (slot_ids[:, None] == jnp.arange(slot_count, dtype=jnp.int32)[None, :]).astype(
        jnp.float32
    )
    chosen = chosen.reshape(tok_rows, top_count, slot_count)
    select = jnp.sum(chosen, axis=1)
    weighted = jnp.sum(chosen * gate_probs[:, :, None], axis=1)
    contract_rows = (((0,), (0,)), ((), ()))
    contract_cols = (((1,), (1,)), ((), ()))
    x_rows = lax.dot_general(
        select.astype(jnp.bfloat16), tokens, contract_rows, preferred_element_type=jnp.float32
    ).astype(jnp.bfloat16)
    back_row = lax.dot_general(
        weighted,
        cotangent.astype(jnp.float32),
        contract_rows,
        precision=lax.Precision.HIGHEST,
        preferred_element_type=jnp.float32,
    ).astype(jnp.bfloat16)
    outbound = jnp.stack([x_rows, back_row], axis=1).reshape(experts, capacity, 2, columns)
    inbound = deliver(outbound).reshape(slot_count, 2, columns)
    x_in = inbound[:, 0]
    d_in = inbound[:, 1]
    gate_mat = w_gate[0]
    up_mat = w_up[0]
    down_mat = w_down[0]
    part_gate = lax.dot_general(x_in, gate_mat, contract_cols, preferred_element_type=jnp.float32)
    part_up = lax.dot_general(x_in, up_mat, contract_cols, preferred_element_type=jnp.float32)
    part_back = lax.dot_general(d_in, down_mat, contract_cols, preferred_element_type=jnp.float32)
    pre_gate, pre_up, back_hidden = (
        lax.psum(part_gate.astype(jnp.bfloat16), "dp").astype(jnp.float32),
        lax.psum(part_up.astype(jnp.bfloat16), "dp").astype(jnp.float32),
        lax.psum(part_back.astype(jnp.bfloat16), "dp").astype(jnp.float32),
    )
    hidden, back_gate, back_up = activate(pre_gate, pre_up, back_hidden)
    expert_out = jnp.dot(hidden, down_mat, preferred_element_type=jnp.float32).astype(jnp.bfloat16)
    back_rows = (
        jnp.dot(back_gate, gate_mat, preferred_element_type=jnp.float32)
        + jnp.dot(back_up, up_mat, preferred_element_type=jnp.float32)
    ).astype(jnp.bfloat16)
    grad_gate = lax.dot_general(
        back_gate, x_in, contract_rows, preferred_element_type=jnp.float32
    ).astype(jnp.bfloat16)
    grad_up = lax.dot_general(
        back_up, x_in, contract_rows, preferred_element_type=jnp.float32
    ).astype(jnp.bfloat16)
    grad_down = lax.dot_general(
        hidden, d_in, contract_rows, preferred_element_type=jnp.float32
    ).astype(jnp.bfloat16)
    homeward = jnp.stack([expert_out, back_rows], axis=1).reshape(experts, capacity, 2, columns)
    returned = deliver(homeward).reshape(slot_count, 2, columns)
    mixed = jnp.dot(
        weighted,
        returned[:, 0].astype(jnp.float32),
        precision=lax.Precision.HIGHEST,
        preferred_element_type=jnp.float32,
    ).astype(jnp.bfloat16)
    grad_tokens = jnp.dot(
        select.astype(jnp.bfloat16), returned[:, 1], preferred_element_type=jnp.float32
    ).astype(jnp.bfloat16)
    return (mixed, grad_tokens, grad_gate[None], grad_up[None], grad_down[None])


def solution(mesh):
    in_specs = (
        P("expert", "dp"),
        P("expert", "dp"),
        P("expert", None),
        P("expert", None),
        P("expert", None, "dp"),
        P("expert", None, "dp"),
        P("expert", None, "dp"),
    )
    out_specs = (
        P("expert", "dp"),
        P("expert", "dp"),
        P("expert", None, "dp"),
        P("expert", None, "dp"),
        P("expert", None, "dp"),
    )
    return jax.shard_map(
        on_device, mesh=mesh, in_specs=in_specs, out_specs=out_specs, check_vma=False
    )
```

profile of v0, /device:TPU:1, one launch (start us, length us, event | category | flops | bytes accessed | tf_op | source)
XLA Modules:
  0.0 158.1 jit_solution(7407230537476773871)
XLA Ops:
  7.2 0.0 copy-start
  7.2 0.0 copy-start.11
  7.2 0.0 all-reduce.3.cloned.1.call-start
  7.2 0.8 copy.34
  8.1 0.1 eq.29
  8.1 0.8 copy.36
  8.9 0.1 fusion.32
  9.0 0.2 reduce_window_sum.11
  9.2 0.2 select_reduce_fusion.1
  9.3 0.1 reduce_sum.30
  9.4 0.2 convert_reduce_fusion
  9.6 1.0 convolution_convert_fusion.7
  10.6 0.1 stack.18
  10.7 0.0 copy-done.11
  10.7 0.4 convolution_convert_fusion.6
  11.1 0.1 stack.19
  11.2 0.7 pad_maximum_fusion
  11.9 38.8 %all_to_all.10 = bf16[128,2,2,512]{3,1,2,0:T(2,128)(2,1)S(1)} all-to-all(bf16[128,2,2,512]{3,1,2,0:T(2,128)(2,1)S(1)} %pad_maximum_fusion), channel_id=1, replica_groups=mesh['dp'=4,'expert'=128] {'expert'}, dimensions={0} | all-to-all | bytes 1048576 | tf_op jit(solution)/shard_map/all_to_all | solution.py:19
  50.7 0.4 copy.39
  51.1 0.7 fusion.40
  51.9 0.0 copy-start.2
  51.9 1.1 copy-done.2
  53.0 0.0 copy-start.1
  53.0 1.1 convolution_convert_fusion.4
  54.1 0.0 copy-done.1
  54.1 1.1 convolution_convert_fusion.5
  55.3 0.0 copy-done
  55.3 1.2 convolution_convert_fusion.3
  56.4 0.0 all-reduce.3.cloned.1.call-update
  56.5 48.8 %all-reduce.3.cloned.1.call-done = (bf16[256,768]{1,0:T(8,128)(2,1)}, bf16[256,768]{1,0:T(8,128)(2,1)}, bf16[256,768]{1,0:T(8,128)(2,1)}) async-done(((bf16[256,768]{1,0:T(8,128)(2,1)}, bf16[256,768]{1,0:T(8,128)(2,1)}, bf16[256,768]{1,0:T(8,128)(2,1)}), (bf16[256,768]{1,0:T(8,128)(2,1)}, bf16[256,768]{1,0:T(8,128)(2,1)}, bf16[256,768]{1,0:T(8,128)(2,1)})) %all-reduce.3.cloned.1.call-update) | async-done | bytes 1179664 | tf_op jit(solution)/shard_map/psum | solution.py:63
  105.2 0.0 copy-start.4
  105.2 0.0 copy-start.5
  105.2 0.0 copy-start.8
  105.2 2.3 %convolution_convert_fusion.8 = bf16[256,512]{1,0:T(8,128)(2,1)} fusion(bf16[1,768,512]{2,1,0:T(8,128)(2,1)S(1)} %copy-done, bf16[256,768]{1,0:T(8,128)(2,1)} %get-tuple-element.7, bf16[256,768]{1,0:T(8,128)(2,1)} %get-tuple-element.9), kind=kOutput, calls=%fused_computation.13 | convolution fusion | flops 203030528 | bytes 1835008 | tf_op jit(solution)/shard_map/dot_general | solution.py:67
  107.6 0.0 copy-done.4
  107.6 0.0 copy-done.5
  107.6 0.0 copy-done.8
  107.6 0.4 fusion.7
  108.0 1.1 stack.21
  109.0 0.0 copy-start.3
  109.0 0.0 copy-start.6
  109.0 0.0 copy-start.9
  109.0 0.4 fusion.17
  109.4 0.7 copy-done.3
  110.1 0.1 copy-done.6
  110.2 0.1 copy-done.9
  110.4 0.4 fusion.3
  110.8 0.1 stack.22
  110.9 1.5 pad_maximum_fusion.1
  112.4 15.5 %all-to-all-start.1 = ((bf16[128,2,2,512]{3,1,2,0:T(2,128)(2,1)}), bf16[128,2,2,512]{3,1,2,0:T(2,128)(2,1)S(1)}, u32[]{:S(2)}, u32[]{:S(2)}) async-start(bf16[128,2,2,512]{3,1,2,0:T(2,128)(2,1)} %pad_maximum_fusion.1), calls=%async_computation.1 | async-start | bytes 1048576 | tf_op jit(solution)/shard_map/all_to_all | solution.py:19
  127.9 0.0 copy-start.7
  127.9 0.0 copy-start.10
  127.9 1.3 fusion
  129.2 0.0 copy-done.7
  129.2 0.0 copy-done.10
  129.2 1.3 fusion.1
  130.5 1.4 fusion.2
  131.9 16.5 %all-to-all-done.1 = bf16[128,2,2,512]{3,1,2,0:T(2,128)(2,1)S(1)} async-done(((bf16[128,2,2,512]{3,1,2,0:T(2,128)(2,1)}), bf16[128,2,2,512]{3,1,2,0:T(2,128)(2,1)S(1)}, u32[]{:S(2)}, u32[]{:S(2)}) %all-to-all-start.1) | async-done | bytes 524320 | tf_op jit(solution)/shard_map/all_to_all | solution.py:19
  148.5 0.4 copy.42
  148.9 0.7 fusion.39
  149.6 0.8 convolution_convert_fusion.9
  150.4 0.8 convolution_convert_fusion.10
  (2 shorter events, 0.1 us)
Async XLA Ops:
  7.2 48.1 %copy-start = (bf16[1,768,512]{2,1,0:T(8,128)(2,1)S(1)}, bf16[1,768,512]{2,1,0:T(8,128)(2,1)}, u32[]{:S(2)}) copy-start(bf16[1,768,512]{2,1,0:T(8,128)(2,1)} %param.13) | copy-start | bytes 2359300
  7.2 3.5 %copy-start.11 = (bf16[16,512]{1,0:T(8,128)(2,1)S(1)}, bf16[16,512]{1,0:T(8,128)(2,1)}, u32[]{:S(2)}) copy-start(bf16[16,512]{1,0:T(8,128)(2,1)} %param.8) | copy-start | bytes 49156
  7.2 98.0 %all-reduce.3.cloned.1.call-start = ((), (), s32[]{:S(2)}) async-start(), calls=%async_computation.2 | async-start | bytes 2359296 | tf_op jit(solution)/shard_map/psum | solution.py:63
  51.9 1.1 copy-start.2
  53.0 1.1 copy-start.1
  105.2 2.4 %copy-start.4 = (bf16[256,768]{1,0:T(8,128)(2,1)S(1)}, bf16[256,768]{1,0:T(8,128)(2,1)}, u32[]{:S(2)}) copy-start(bf16[256,768]{1,0:T(8,128)(2,1)} %get-tuple-element.7) | copy-start | bytes 1179652
  105.2 2.4 %copy-start.5 = (bf16[256,768]{1,0:T(8,128)(2,1)S(1)}, bf16[256,768]{1,0:T(8,128)(2,1)}, u32[]{:S(2)}) copy-start(bf16[256,768]{1,0:T(8,128)(2,1)} %get-tuple-element.9) | copy-start | bytes 1179652
  105.2 2.4 %copy-start.8 = (bf16[256,768]{1,0:T(8,128)(2,1)S(1)}, bf16[256,768]{1,0:T(8,128)(2,1)}, u32[]{:S(2)}) copy-start(bf16[256,768]{1,0:T(8,128)(2,1)} %get-tuple-element.8) | copy-start | bytes 1179652
  109.0 1.1 copy-start.3
  109.0 1.2 copy-start.6
  109.0 1.3 copy-start.9
  112.4 36.1 %all-to-all-start.1 = ((bf16[128,2,2,512]{3,1,2,0:T(2,128)(2,1)}), bf16[128,2,2,512]{3,1,2,0:T(2,128)(2,1)S(1)}, u32[]{:S(2)}, u32[]{:S(2)}) async-start(bf16[128,2,2,512]{3,1,2,0:T(2,128)(2,1)} %pad_maximum_fusion.1), calls=%async_computation.1 | async-start | bytes 1048576 | tf_op jit(solution)/shard_map/all_to_all | solution.py:19
  127.9 1.3 copy-start.7
  127.9 1.3 copy-start.10
Sparse Core Ops, SparseCore 0:
  56.6 48.5 all-reduce.2
where the time goes:
time: 158 us
  waiting for transfers between devices  65.3 us (41%)
  blocking collectives  38.8 us (25%)
  starting transfers between devices  15.6 us (10%)
  between operations  14.2 us (9%)
  matrix products  13.5 us (9%)
  local copies, waits for them, and re-layouts  7.51 us (5%)
  other arithmetic  3.1 us (2%)
    psum x1, waiting for transfers between devices, on_device(): lax.psum(part_up.astype(jnp.bfloat16), 'dp').astype(jnp.float32)  48.8 us
    all_to_all x1, blocking collectives, deliver(): lax.all_to_all(outbound, 'expert', split_axis=0, concat_axis=0, tiled=True)  38.8 us
    all_to_all x1, waiting for transfers between devices, deliver(): lax.all_to_all(outbound, 'expert', split_axis=0, concat_axis=0, tiled=True)  16.5 us
    all_to_all x1, starting transfers between devices, deliver(): lax.all_to_all(outbound, 'expert', split_axis=0, concat_axis=0, tiled=True)  15.5 us
    unnamed x27, local copies, waits for them, and re-layouts  3.7 us
  transfers between devices with their start and end apart: 2, of which 2 were waited for; matrix products, arithmetic and copies ran while one was open for 3% of the time, Pallas kernels for 0%

commit v1 on v0

--- a/solution.py
+++ b/solution.py
@@ -1,6 +1,8 @@
 import jax
 import jax.numpy as jnp
 from jax import lax
+from jax.experimental import pallas as pl
+from jax.experimental.pallas import tpu as pltpu
 from jax.sharding import PartitionSpec as P
 
 
@@ -15,8 +17,79 @@
     return (hidden, back_gate, back_up)
 
 
+MESH = pl.DeviceIdType.MESH
+
+
+def wait_bytes(ref, sem):
+    pltpu.make_async_copy(ref, ref, sem).wait()
+
+
+def exchange(src, dst, send_sem, recv_sem, local_sem, ready):
+    x, e = lax.axis_index("dp"), lax.axis_index("expert")
+    z, y, c = e // 16, (e // 2) % 8, e % 2
+
+    def peer(dz, dy, dc):
+        return lax.rem(z + dz, 8) * 16 + lax.rem(y + dy, 8) * 2 + lax.rem(c + dc, 2)
+
+    def greet(sem, dz, dy, dc):
+        pl.semaphore_signal(sem, inc=1, device_id=(x, peer(dz, dy, dc)), device_id_type=MESH)
+
+    def send(dz, dy, dc):
+        p = peer(dz, dy, dc)
+        pltpu.make_async_remote_copy(
+            src_ref=src.at[p],
+            dst_ref=dst.at[e],
+            send_sem=send_sem,
+            recv_sem=recv_sem,
+            device_id=(x, p),
+            device_id_type=MESH,
+        ).start()
+
+    barrier = pltpu.get_barrier_semaphore()
+    for dz in range(1, 8):
+        greet(barrier, dz, 0, 0)
+    for i in range(1, 16):
+        greet(barrier, 0, i // 2, i % 2)
+    keep = pltpu.make_async_copy(src.at[e], dst.at[e], local_sem)
+    keep.start()
+    pl.semaphore_wait(barrier, 22)
+    for dz in range(1, 8):
+        greet(ready, dz, 0, 0)
+    for i in range(1, 16):
+        send(0, i // 2, i % 2)
+    for dz in range(1, 8):
+        send(dz, 0, 0)
+    pl.semaphore_wait(ready, 7)
+
+    def far(i, carry):
+        i = lax.rem(i * 11, 105)
+        j = i % 15 + 1
+        send(i // 15 + 1, j // 2, j % 2)
+        return carry
+
+    lax.fori_loop(0, 105, far, 0)
+    keep.wait()
+    wait_bytes(src.at[pl.ds(0, 127)], send_sem)
+    wait_bytes(dst.at[pl.ds(0, 127)], recv_sem)
+
+
 def deliver(outbound):
-    return lax.all_to_all(outbound, "expert", split_axis=0, concat_axis=0, tiled=True)
+    shape = outbound.shape
+    flat = outbound.reshape(128, 16, 128)
+    out = pl.pallas_call(
+        exchange,
+        out_shape=jax.ShapeDtypeStruct(flat.shape, flat.dtype),
+        in_specs=[pl.BlockSpec(memory_space=pltpu.VMEM)],
+        out_specs=pl.BlockSpec(memory_space=pltpu.VMEM),
+        scratch_shapes=[
+            pltpu.SemaphoreType.DMA,
+            pltpu.SemaphoreType.DMA,
+            pltpu.SemaphoreType.DMA,
+            pltpu.SemaphoreType.REGULAR,
+        ],
+        compiler_params=pltpu.CompilerParams(collective_id=0, has_side_effects=True),
+    )(flat)
+    return out.reshape(shape)
 
 
 def on_device(tokens, cotangent, expert_ids, gate_probs, w_gate, w_up, w_down):

time: 158 us -> 153 us (0.968)
  Pallas kernels: 0 us -> 60.9 us
  blocking collectives: 38.8 us -> 0 us
  starting transfers between devices: 15.6 us -> 0.04 us
  waiting for transfers between devices: 65.3 us -> 52.1 us
  local copies, waits for them, and re-layouts: 7.51 us -> 10.7 us
  other arithmetic: 3.1 us -> 1.06 us
    pallas_call x0 -> x2, Pallas kernels: none -> 60.9 us  [deliver(): pl.pallas_call(exchange, out_shape=jax.ShapeDtypeStruct(flat.shape, flat....]
    all_to_all x1 -> x0, blocking collectives: 38.8 us -> none  [deliver(): lax.all_to_all(outbound, 'expert', split_axis=0, concat_axis=0, tiled=True)]
    all_to_all x1 -> x0, waiting for transfers between devices: 16.5 us -> none  [deliver(): lax.all_to_all(outbound, 'expert', split_axis=0, concat_axis=0, tiled=True)]
    all_to_all x1 -> x0, starting transfers between devices: 15.5 us -> none  [deliver(): lax.all_to_all(outbound, 'expert', split_axis=0, concat_axis=0, tiled=True)]
    another operation x0 -> x4, local copies, waits for them, and re-layouts: none -> 4.73 us  [the longest x2 2.25 us: deliver(): flat = outbound.reshape(128, 16, 128)]
    psum x1, waiting for transfers between devices: 48.8 us -> 52.1 us  [on_device(): lax.psum(part_up.astype(jnp.bfloat16), 'dp').astype(jnp.float32)]
    dot_general x1, matrix products: 2.34 us -> 0.43 us  [on_device(): jnp.dot(hidden, down_mat, preferred_element_type=jnp.float32)]
    unnamed x27 -> x15, local copies, waits for them, and re-layouts: 3.7 us -> 3.27 us
  transfers between devices with their start and end apart: 2 -> 1, of which waited for: 2 -> 1; matrix products, arithmetic and copies ran while one was open for 3% -> 0% of each run, Pallas kernels for 0% -> 0%
where the time goes in v1:
time: 153 us
  Pallas kernels  60.9 us (40%)
  waiting for transfers between devices  52.1 us (34%)
  between operations  14.2 us (9%)
  matrix products  13.5 us (9%)
  local copies, waits for them, and re-layouts  10.7 us (7%)
    pallas_call x2, Pallas kernels, deliver(): pl.pallas_call(exchange, out_shape=jax.ShapeDtypeStruct(flat.shape, flat....  60.9 us
    psum x1, waiting for transfers between devices, on_device(): lax.psum(part_up.astype(jnp.bfloat16), 'dp').astype(jnp.float32)  52.1 us
    unnamed x15, local copies, waits for them, and re-layouts  3.27 us
  transfers between devices with their start and end apart: 1, of which 1 were waited for; matrix products, arithmetic and copies ran while one was open for 0% of the time, Pallas kernels for 0%

profile of v1, /device:TPU:1, one launch (start us, length us, event | category | flops | bytes accessed | tf_op | source)
XLA Modules:
  0.0 152.6 jit_solution(15710164123851877587)
XLA Ops:
  7.2 0.0 copy-start
  7.2 0.0 all-reduce.3.cloned.1.call-start
  7.2 0.8 copy.26
  8.0 0.1 eq.29
  8.1 0.8 copy.28
  8.9 0.1 fusion.24
  9.0 0.2 reduce_window_sum.11
  9.2 0.2 select_reduce_fusion.1
  9.3 0.1 reduce_sum.30
  9.4 0.2 convert_reduce_fusion
  9.6 1.0 fusion.6
  10.6 1.1 fusion.7
  11.7 0.1 pad_maximum_fusion
  11.8 0.5 copy.29
  12.3 1.1 reshape_reshape.12.src
  13.5 32.8 %shard_map.110 = bf16[128,16,128]{2,1,0:T(8,128)(2,1)} custom-call(bf16[128,16,128]{2,1,0:T(8,128)(2,1)} %reshape_reshape.12.src), custom_call_target="tpu_custom_call" | custom-call | tf_op jit(solution)/shard_map/pallas_call | solution.py:79
  46.2 1.2 reshape_reshape.13
  47.5 0.7 fusion.32
  48.2 0.0 copy-start.2
  48.3 0.0 copy-start.1
  48.3 1.1 copy-done.2
  49.4 1.1 convolution_convert_fusion.4
  50.5 0.0 copy-done.1
  50.5 1.2 convolution_convert_fusion.5
  51.7 0.0 copy-done
  51.7 1.2 convolution_convert_fusion.3
  52.8 0.0 all-reduce.3.cloned.1.call-update
  52.8 52.1 %all-reduce.3.cloned.1.call-done = (bf16[256,768]{1,0:T(8,128)(2,1)}, bf16[256,768]{1,0:T(8,128)(2,1)}, bf16[256,768]{1,0:T(8,128)(2,1)}) async-done(((bf16[256,768]{1,0:T(8,128)(2,1)}, bf16[256,768]{1,0:T(8,128)(2,1)}, bf16[256,768]{1,0:T(8,128)(2,1)}), (bf16[256,768]{1,0:T(8,128)(2,1)}, bf16[256,768]{1,0:T(8,128)(2,1)}, bf16[256,768]{1,0:T(8,128)(2,1)})) %all-reduce.3.cloned.1.call-update) | async-done | bytes 1179664 | tf_op jit(solution)/shard_map/psum | solution.py:136
  105.0 0.0 copy-start.4
  105.0 0.0 copy-start.5
  105.0 2.6 %fusion.2 = bf16[1,768,512]{2,1,0:T(8,128)(2,1)} fusion(bf16[256,1,512]{2,1,0:T(2,128)(2,1)S(1)} %get-tuple-element.12, bf16[256,768]{1,0:T(8,128)(2,1)} %get-tuple-element.7, bf16[256,768]{1,0:T(8,128)(2,1)} %get-tuple-element.9), kind=kOutput, calls=%fused_computation.5 | convolution fusion | flops 203292672 | bytes 1835008 | tf_op jit(solution)/shard_map/dot_general | solution.py:151
  107.5 0.0 copy-done.4
  107.5 0.0 copy-done.5
  107.5 0.0 copy-start.3
  107.6 0.4 fusion.4
  108.0 0.6 copy-done.3
  108.5 0.4 fusion.11
  108.9 1.3 fusion.1
  110.2 0.4 fusion.21
  110.6 1.3 fusion
  111.9 0.4 fusion.5
  112.3 0.1 pad_maximum_fusion.1
  112.4 0.5 copy.32
  112.9 1.1 reshape_reshape.14.src
  114.0 28.1 %shard_map.111 = bf16[128,16,128]{2,1,0:T(8,128)(2,1)} custom-call(bf16[128,16,128]{2,1,0:T(8,128)(2,1)} %reshape_reshape.14.src), custom_call_target="tpu_custom_call" | custom-call | tf_op jit(solution)/shard_map/pallas_call | solution.py:79
  142.2 1.2 reshape_reshape.15
  143.4 0.7 fusion.31
  144.1 0.8 convolution_convert_fusion.9
  144.9 0.8 convolution_convert_fusion.10
  (2 shorter events, 0.1 us)
Async XLA Ops:
  7.2 44.5 %copy-start = (bf16[1,768,512]{2,1,0:T(8,128)(2,1)S(1)}, bf16[1,768,512]{2,1,0:T(8,128)(2,1)}, u32[]{:S(2)}) copy-start(bf16[1,768,512]{2,1,0:T(8,128)(2,1)} %param.13) | copy-start | bytes 2359300
  7.2 97.8 %all-reduce.3.cloned.1.call-start = ((), (), s32[]{:S(2)}) async-start(), calls=%async_computation | async-start | bytes 2359296 | tf_op jit(solution)/shard_map/psum | solution.py:136
  48.2 1.1 copy-start.2
  48.3 2.2 %copy-start.1 = (bf16[1,768,512]{2,1,0:T(8,128)(2,1)S(1)}, bf16[1,768,512]{2,1,0:T(8,128)(2,1)}, u32[]{:S(2)}) copy-start(bf16[1,768,512]{2,1,0:T(8,128)(2,1)} %param.11) | copy-start | bytes 2359300
  105.0 2.6 %copy-start.4 = (bf16[256,768]{1,0:T(8,128)(2,1)S(1)}, bf16[256,768]{1,0:T(8,128)(2,1)}, u32[]{:S(2)}) copy-start(bf16[256,768]{1,0:T(8,128)(2,1)} %get-tuple-element.9) | copy-start | bytes 1179652
  105.0 2.6 %copy-start.5 = (bf16[256,768]{1,0:T(8,128)(2,1)S(1)}, bf16[256,768]{1,0:T(8,128)(2,1)}, u32[]{:S(2)}) copy-start(bf16[256,768]{1,0:T(8,128)(2,1)} %get-tuple-element.7) | copy-start | bytes 1179652
  107.5 1.0 copy-start.3
Sparse Core Ops, SparseCore 0:
  53.0 51.9 all-reduce.2

commit v2 on v0

v2 whole, which is shorter than its diff:
```python
import functools

import jax
import jax.numpy as jnp
from jax import lax
from jax.experimental import pallas as pl
from jax.experimental.pallas import tpu as pltpu
from jax.sharding import PartitionSpec as P

MESH = pl.DeviceIdType.MESH
BF16 = jnp.bfloat16
F32 = jnp.float32
CHUNKS = 4
SOURCES = 128 // CHUNKS
ROWS = 2 * SOURCES
PIECE = ROWS // 4
ORDER = (0, 1, 7, 2, 6, 3, 5, 4)
COLUMNS = 512
FF = 768
WIDE = 3 * FF
HALF = WIDE // 2


def wait_bytes(ref, sem):
    pltpu.make_async_copy(ref, ref, sem).wait()


def dot(a, b):
    return jnp.dot(a, b, preferred_element_type=F32)


def dot_nt(a, b):
    return lax.dot_general(a, b, (((1,), (1,)), ((), ())), preferred_element_type=F32)


def iota(shape, axis):
    return lax.broadcasted_iota(jnp.int32, shape, axis)


def routed(
    ids_ref,
    probs_ref,
    tokens_ref,
    cot_ref,
    gate_hbm,
    up_hbm,
    down_hbm,
    mixed_ref,
    grad_ref,
    xin,
    acts,
    gate_ref,
    up_ref,
    down_ref,
    out_box,
    in_box,
    home_box,
    back_box,
    back_hi,
    back_lo,
    spread,
    gather,
    part,
    first_in,
    second_out,
    second_in,
    load_sem,
    local_sem,
    send_sem,
    recv_sem,
    home_send,
    home_recv,
    ring_send,
    ring_recv,
    ready,
):
    x, e = lax.axis_index("dp"), lax.axis_index("expert")
    z, yc = e // 16, e % 16
    y, c = yc // 2, yc % 2
    right, left = lax.rem(x + 1, 4), lax.rem(x + 3, 4)
    opposite = lax.rem(x + 2, 4)
    sides = ((right, e), (left, e))
    near = (right, left)

    def plane(d, row):
        return (x, lax.rem(z + d, 8) * 16 + row)

    def greet(sem, device):
        pl.semaphore_signal(sem, inc=1, device_id=device, device_id_type=MESH)

    def push(src, dst, ssem, rsem, device):
        copy = pltpu.make_async_remote_copy(
            src_ref=src,
            dst_ref=dst,
            send_sem=ssem,
            recv_sem=rsem,
            device_id=device,
            device_id_type=MESH,
        )
        copy.start()
        return copy

    barrier = pltpu.get_barrier_semaphore()
    for side in sides:
        greet(barrier, side)
    for d in range(1, 8):
        greet(barrier, plane(d, yc))
    for i in range(1, 16):
        greet(barrier, plane(0, lax.rem(yc + i, 16)))
    loads = []
    for i, (src, dst) in enumerate(
        ((gate_hbm, gate_ref), (up_hbm, up_ref), (down_hbm, down_ref))
    ):
        load = pltpu.make_async_copy(src.at[0], dst, load_sem.at[i])
        load.start()
        loads.append(load)

    lane = iota((16, 128), 1)
    own_token = iota((16, 128), 0) == lane % 16
    ids = ids_ref[...].astype(F32)
    probs = probs_ref[...]
    rows = iota((128, 128), 0)
    cols = iota((128, 128), 1)
    turn = rows // 16
    step = jnp.where(turn % 2 == 1, (turn + 1) // 2, (8 - turn // 2) % 8)
    expert = ((z + step) % 8 * 16 + rows % 16).astype(F32)
    taken = jnp.zeros((128, 128), F32)
    weight = jnp.zeros((128, 128), F32)
    for k in range(8):
        id_row = jnp.sum(jnp.where(own_token, ids[:, k : k + 1], 0.0), axis=0, keepdims=True)
        prob_row = jnp.sum(
            jnp.where(own_token, probs[:, k : k + 1], 0.0), axis=0, keepdims=True
        )
        same = expert == id_row
        taken = jnp.where(same, 1.0, taken)
        weight = jnp.where(same, prob_row, weight)
    earlier = ((rows // 16 == cols // 16) & (rows < cols)).astype(F32).astype(BF16)
    rank = dot(taken.astype(BF16), earlier)
    code = jnp.where(taken > 0.0, (cols // 16 * 2).astype(F32) + rank, -1.0)
    feature = cols < 64
    out_value = jnp.where(feature, taken, weight)
    back_value = jnp.where(feature, weight, taken)
    out_high = out_value.astype(BF16).astype(F32)
    back_high = back_value.astype(BF16).astype(F32)
    out_low, back_low = out_value - out_high, back_value - back_high

    tokens = tokens_ref[...]
    cot = cot_ref[...]
    features = jnp.concatenate(
        [tokens[:, g * 128 : (g + 1) * 128] for g in range(4)]
        + [cot[:, g * 128 : (g + 1) * 128] for g in range(4)],
        axis=0,
    )
    slot = iota((16, 16, 128), 1).astype(F32)

    def expand(value, mine):
        full = jnp.where(mine, value[:, None, :], 0.0)
        return full.reshape(256, 128)

    for q in range(8):
        part_rows = slice(16 * q, 16 * (q + 1))
        mine = code[part_rows][:, None, :] == slot
        high = expand(out_high[part_rows], mine).astype(BF16)
        low = expand(out_low[part_rows], mine).astype(BF16)
        sent = dot(high, features) + dot(low, features)
        out_box[q] = sent.astype(BF16).reshape(16, 16, 128)

    pl.semaphore_wait(barrier, 24)
    for d in range(1, 8):
        greet(ready, plane(d, yc))
    keep = pltpu.make_async_copy(out_box.at[0, yc], in_box.at[0, yc], local_sem.at[0])
    keep.start()

    def send_to(q, i):
        row = lax.rem(yc + i, 16)
        k, j = q // (8 // CHUNKS), q % (8 // CHUNKS)
        push(
            out_box.at[q, row],
            in_box.at[k, j * 16 + yc],
            send_sem,
            recv_sem.at[k],
            plane(ORDER[q], row),
        )

    def send_group(q, first):
        def body(i, carry):
            send_to(q, i)
            return carry

        lax.fori_loop(first, 16, body, 0)

    send_group(0, 1)
    pl.semaphore_wait(ready, 7)
    for q in range(1, 8):
        send_group(q, 0)

    for q in range(8):
        part_rows = slice(16 * q, 16 * (q + 1))
        mine = code[part_rows][:, None, :] == slot
        high = expand(back_high[part_rows], mine)
        low = expand(back_low[part_rows], mine)
        back_hi[:, q * 256 : (q + 1) * 256] = high.T.astype(BF16)
        back_lo[:, q * 256 : (q + 1) * 256] = low.T.astype(BF16)
    big_row, big_col = iota((256, 256), 0), iota((256, 256), 1)
    gather[...] = (
        (big_row // 32 == big_col % 16 // 2)
        & (big_row % 32 // 2 == big_col // 16)
        & (big_row % 2 == big_col % 2)
    ).astype(F32).astype(BF16)
    spread[...] = (
        (big_col // 32 == big_row % 16 // 2)
        & (big_col % 32 // 2 == big_row // 16)
        & (big_row % 2 == big_col % 2)
    ).astype(F32).astype(BF16)
    for load in loads:
        load.wait()
    keep.wait()

    ring = {}

    def hop(stage, k, i, src, dst):
        ring[stage, k, i] = push(
            src, dst, ring_send.at[stage, k, i], ring_recv.at[stage, k, i], sides[i]
        )

    def halves(i):
        return pl.ds(HALF * i, HALF)

    def stage_partial(k):
        if k == 0:
            wait_bytes(in_box.at[0, pl.ds(0, SOURCES - 1)], recv_sem.at[0])
        else:
            wait_bytes(in_box.at[k], recv_sem.at[k])
        for a in range(SOURCES // 16):
            block = in_box[k, 16 * a : 16 * (a + 1)].reshape(256, 128)
            ordered = dot(gather[...], block).astype(BF16)
            for g in range(8):
                xin[k, 32 * a : 32 * (a + 1), g * 128 : (g + 1) * 128] = ordered[
                    32 * g : 32 * (g + 1)
                ]
        x_rows = xin[k, :, :COLUMNS]
        d_rows = xin[k, :, COLUMNS:]
        for n, (rows_in, ref) in enumerate(
            ((x_rows, gate_ref), (x_rows, up_ref), (d_rows, down_ref))
        ):
            value = dot_nt(rows_in, ref[...]).astype(BF16)
            part[k, :, :, n * FF : (n + 1) * FF] = value.reshape(4, PIECE, FF)
        for i in range(2):
            hop(0, k, i, part.at[k, opposite, :, halves(i)], first_in.at[k, :, halves(i)])

    def stage_sum(k):
        for i in range(2):
            ring[0, k, i].wait_recv()
        for i in range(2):
            span = slice(HALF * i, HALF * (i + 1))
            rest = slice(HALF * (1 - i), HALF * (2 - i))
            second_out[k, i, :, span] = (
                part[k, near[i], :, span].astype(F32) + first_in[k, :, span].astype(F32)
            ).astype(BF16)
            second_out[k, i, :, rest] = part[k, near[i], :, rest]
        for i in range(2):
            hop(1, k, i, second_out.at[k, i], second_in.at[k, i])

    def stage_act(k):
        for i in range(2):
            ring[1, k, i].wait_recv()

        def total(n):
            span = slice(n * FF, (n + 1) * FF)
            return (
                part[k, x, :, span].astype(F32)
                + second_in[k, 0, :, span].astype(F32)
                + second_in[k, 1, :, span].astype(F32)
            )

        gate, up, back = total(0), total(1), total(2)
        sig = jax.nn.sigmoid(gate)
        silu = gate * sig
        acts[k, x, :, :FF] = (silu * up).astype(BF16)
        acts[k, x, :, FF : 2 * FF] = (
            back * up * sig * (1.0 + gate * (1.0 - sig))
        ).astype(BF16)
        acts[k, x, :, 2 * FF :] = (back * silu).astype(BF16)
        for i in range(2):
            hop(2, k, i, acts.at[k, x], acts.at[k, x])

    def stage_forward(k):
        for i in range(2):
            ring[2, k, i].wait_recv()
        for i in range(2):
            piece = acts.at[k, near[1 - i], :, halves(i)]
            hop(3, k, i, piece, piece)

    def stage_home(k):
        for i in range(2):
            ring[3, k, i].wait_recv()
        h = acts[k].reshape(ROWS, WIDE)
        out = dot(h[:, :FF], down_ref[...]).astype(BF16)
        back = (
            dot(h[:, FF : 2 * FF], gate_ref[...]) + dot(h[:, 2 * FF :], up_ref[...])
        ).astype(BF16)
        for a in range(SOURCES // 16):
            span = slice(32 * a, 32 * (a + 1))
            stack = jnp.concatenate(
                [out[span, g * 128 : (g + 1) * 128] for g in range(4)]
                + [back[span, g * 128 : (g + 1) * 128] for g in range(4)],
                axis=0,
            )
            home_box[k, 16 * a : 16 * (a + 1)] = (
                dot(spread[...], stack).astype(BF16).reshape(16, 16, 128)
            )
        for j in range(8 // CHUNKS):
            q = k * (8 // CHUNKS) + j

            def body(i, carry, j=j, q=q):
                row = lax.rem(yc + i, 16)
                push(
                    home_box.at[k, j * 16 + row],
                    back_box.at[k, j * 16 + yc],
                    home_send,
                    home_recv.at[k],
                    plane(8 - ORDER[q], row),
                )
                return carry

            lax.fori_loop(1 if q == 0 else 0, 16, body, 0)
        if k == 0:
            copy = pltpu.make_async_copy(
                home_box.at[0, yc], back_box.at[0, yc], local_sem.at[1]
            )
            copy.start()
            ring["home"] = copy

    stages = (stage_partial, stage_sum, stage_act, stage_forward, stage_home)
    for t in range(CHUNKS + len(stages) - 1):
        for s in reversed(range(len(stages))):
            if 0 <= t - s < CHUNKS:
                stages[s](t - s)

    total = jnp.zeros((128, 128), F32)
    for k in range(CHUNKS):
        if k == 0:
            ring["home"].wait()
            wait_bytes(back_box.at[0, pl.ds(0, SOURCES - 1)], home_recv.at[0])
        else:
            wait_bytes(back_box.at[k], home_recv.at[k])
        block = back_box[k].reshape(SOURCES * 16, 128)
        span = slice(k * SOURCES * 16, (k + 1) * SOURCES * 16)
        total = total + dot(back_hi[:, span], block) + dot(back_lo[:, span], block)
    result = total.astype(BF16)
    for g in range(4):
        mixed_ref[:, g * 128 : (g + 1) * 128] = result[16 * g : 16 * (g + 1)]
        grad_ref[:, g * 128 : (g + 1) * 128] = result[64 + 16 * g : 64 + 16 * (g + 1)]

    for stage in range(4):
        for k in range(CHUNKS):
            for i in range(2):
                ring[stage, k, i].wait_send()
    wait_bytes(out_box.at[pl.ds(0, 7)], send_sem)
    wait_bytes(out_box.at[0, pl.ds(0, 15)], send_sem)
    wait_bytes(back_box.at[pl.ds(0, CHUNKS - 1)], home_send)
    wait_bytes(back_box.at[0, pl.ds(0, SOURCES - 1)], home_send)


def on_device(tokens, cotangent, expert_ids, gate_probs, w_gate, w_up, w_down):
    vmem = pl.BlockSpec(memory_space=pltpu.VMEM)
    hbm = pl.BlockSpec(memory_space=pl.ANY)

    def buf(*shape):
        return pltpu.VMEM(shape, BF16)

    dma = pltpu.SemaphoreType.DMA
    mixed, grad_tokens, xin, acts = pl.pallas_call(
        routed,
        out_shape=(
            jax.ShapeDtypeStruct((16, COLUMNS), BF16),
            jax.ShapeDtypeStruct((16, COLUMNS), BF16),
            jax.ShapeDtypeStruct((CHUNKS, ROWS, 2 * COLUMNS), BF16),
            jax.ShapeDtypeStruct((CHUNKS, 4, PIECE, WIDE), BF16),
        ),
        in_specs=[vmem] * 4 + [hbm] * 3,
        out_specs=(vmem, vmem, vmem, vmem),
        scratch_shapes=[
            buf(FF, COLUMNS),
            buf(FF, COLUMNS),
            buf(FF, COLUMNS),
            buf(8, 16, 16, 128),
            buf(CHUNKS, SOURCES, 16, 128),
            buf(CHUNKS, SOURCES, 16, 128),
            buf(CHUNKS, SOURCES, 16, 128),
            buf(128, 2048),
            buf(128, 2048),
            buf(256, 256),
            buf(256, 256),
            buf(CHUNKS, 4, PIECE, WIDE),
            buf(CHUNKS, PIECE, WIDE),
            buf(CHUNKS, 2, PIECE, WIDE),
            buf(CHUNKS, 2, PIECE, WIDE),
            dma((3,)),
            dma((2,)),
            dma,
            dma((CHUNKS,)),
            dma,
            dma((CHUNKS,)),
            dma((4, CHUNKS, 2)),
            dma((4, CHUNKS, 2)),
            pltpu.SemaphoreType.REGULAR,
        ],
        compiler_params=pltpu.CompilerParams(
            collective_id=0, has_side_effects=True, vmem_limit_bytes=60 * 1024 * 1024
        ),
    )(expert_ids, gate_probs, tokens, cotangent, w_gate, w_up, w_down)
    x_in = xin.reshape(256, 2 * COLUMNS)
    h = acts.reshape(256, WIDE)
    over_rows = (((0,), (0,)), ((), ()))

    def outer(a, b):
        return lax.dot_general(a, b, over_rows, preferred_element_type=F32).astype(BF16)[None]

    grad_gate = outer(h[:, FF : 2 * FF], x_in[:, :COLUMNS])
    grad_up = outer(h[:, 2 * FF :], x_in[:, :COLUMNS])
    grad_down = outer(h[:, :FF], x_in[:, COLUMNS:])
    return (mixed, grad_tokens, grad_gate, grad_up, grad_down)


def solution(mesh):
    in_specs = (
        P("expert", "dp"),
        P("expert", "dp"),
        P("expert", None),
        P("expert", None),
        P("expert", None, "dp"),
        P("expert", None, "dp"),
        P("expert", None, "dp"),
    )
    out_specs = (
        P("expert", "dp"),
        P("expert", "dp"),
        P("expert", None, "dp"),
        P("expert", None, "dp"),
        P("expert", None, "dp"),
    )
    return jax.shard_map(
        on_device, mesh=mesh, in_specs=in_specs, out_specs=out_specs, check_vma=False
    )
```

time: 158 us -> 81.8 us (0.52)
  Pallas kernels: 0 us -> 70.9 us
  waiting for transfers between devices: 65.3 us -> 0 us
  blocking collectives: 38.8 us -> 0 us
  starting transfers between devices: 15.6 us -> 0 us
  between operations: 14.2 us -> 0.66 us
  matrix products: 13.5 us -> 5.98 us
  local copies, waits for them, and re-layouts: 7.51 us -> 3.94 us
  other arithmetic: 3.1 us -> 0 us
    pallas_call x0 -> x1, Pallas kernels: none -> 70.9 us  [on_device(): pl.pallas_call(routed, out_shape=(jax.ShapeDtypeStruct((16, COLUMNS), BF1...]
    psum x1 -> x0, waiting for transfers between devices: 48.8 us -> none  [on_device(): lax.psum(part_up.astype(jnp.bfloat16), 'dp').astype(jnp.float32)]
    all_to_all x1 -> x0, blocking collectives: 38.8 us -> none  [deliver(): lax.all_to_all(outbound, 'expert', split_axis=0, concat_axis=0, tiled=True)]
    all_to_all x1 -> x0, waiting for transfers between devices: 16.5 us -> none  [deliver(): lax.all_to_all(outbound, 'expert', split_axis=0, concat_axis=0, tiled=True)]
    all_to_all x1 -> x0, starting transfers between devices: 15.5 us -> none  [deliver(): lax.all_to_all(outbound, 'expert', split_axis=0, concat_axis=0, tiled=True)]
    dot_general x13 -> x3, matrix products: 13.5 us -> 5.98 us  [outer(): lax.dot_general(a, b, over_rows, preferred_element_type=F32).astype(BF16)]
    another operation x3 -> x0, other arithmetic: 2.32 us -> none  [the longest x1 1.47 us: on_device(): jnp.stack([expert_out, back_rows], axis=1)]
    unnamed x27 -> x12, local copies, waits for them, and re-layouts: 3.7 us -> 3.94 us
  transfers between devices with their start and end apart: 2 -> 0, of which waited for: 2 -> 0; matrix products, arithmetic and copies ran while one was open for 3% -> 0% of each run, Pallas kernels for 0% -> 0%
where the time goes in v2:
time: 81.8 us; the launch traced here: 81.5 us
  Pallas kernels  70.9 us (87%)
  matrix products  5.98 us (7%)
  local copies, waits for them, and re-layouts  3.94 us (5%)
    pallas_call x1, Pallas kernels, on_device(): pl.pallas_call(routed, out_shape=(jax.ShapeDtypeStruct((16, COLUMNS), BF1...  70.9 us
    dot_general x3, matrix products, outer(): lax.dot_general(a, b, over_rows, preferred_element_type=F32).astype(BF16)  5.98 us
    unnamed x12, local copies, waits for them, and re-layouts  3.94 us

profile of v2, /device:TPU:1, one launch (start us, length us, event | category | flops | bytes accessed | tf_op | source)
XLA Modules:
  0.0 81.5 jit_solution(247367063580488432)
XLA Ops:
  0.6 1.4 %copy.12.ids_ref = s32[16,8]{1,0:T(8,128)} copy(s32[16,8]{0,1:T(8,128)} %param.9) | data formatting | bytes 1024 | tf_op args[2]
  2.0 1.4 %copy.13.probs_ref = f32[16,8]{1,0:T(8,128)} copy(f32[16,8]{0,1:T(8,128)} %param.10) | data formatting | bytes 1024 | tf_op args[3]
  3.3 70.9 %shard_map.110 = (bf16[16,512]{1,0:T(8,128)(2,1)}, bf16[16,512]{1,0:T(8,128)(2,1)}, bf16[4,64,1024]{2,1,0:T(8,128)(2,1)}, bf16[4,4,16,2304]{3,2,1,0:T(8,128)(2,1)}) custom-call(s32[16,8]{1,0:T(8,128)} %copy.12.ids_ref, f32[16,8]{1,0:T(8,128)} %copy.13.probs_ref, bf16[16,512]{1,0:T(8,128)(2,1)} %tokens_ref.1, bf16[16,512]{1,0:T(8,128)(2,1)} %cot_ref.1, ...), custom_call_target="tpu_custom_call" | custom-call | tf_op jit(solution)/shard_map/pallas_call | solution.py:373
  74.2 0.0 copy-start
  74.2 0.0 copy-start.1
  74.2 2.5 %fusion.2 = bf16[1,768,512]{2,1,0:T(8,128)(2,1)} fusion(bf16[256,2304]{1,0:T(8,128)(2,1)} %bitcast.8, bf16[256,1024]{1,0:T(8,128)(2,1)} %bitcast.11), kind=kOutput, calls=%fused_computation.5 | convolution fusion | flops 201719808 | bytes 1441792 | tf_op jit(solution)/shard_map/dot_general | solution.py:418
  76.7 0.0 copy-done
  76.7 0.0 copy-start.3
  76.7 0.0 copy-start.2
  76.7 2.2 %fusion.1 = bf16[1,768,512]{2,1,0:T(8,128)(2,1)} fusion(bf16[256,2304]{1,0:T(8,128)(2,1)S(1)} %bitcast.9, bf16[256,1024]{1,0:T(8,128)(2,1)} %bitcast.12), kind=kOutput, calls=%fused_computation.4 | convolution fusion | flops 201719808 | bytes 1441792 | tf_op jit(solution)/shard_map/dot_general | solution.py:418
  79.0 0.0 copy-done.1
  79.0 1.3 %fusion = bf16[1,768,512]{2,1,0:T(8,128)(2,1)} fusion(bf16[256,2304]{1,0:T(8,128)(2,1)S(1)} %bitcast.10, bf16[256,1024]{1,0:T(8,128)(2,1)S(1)} %bitcast.13), kind=kOutput, calls=%fused_computation.3 | convolution fusion | flops 201719808 | bytes 1441792 | tf_op jit(solution)/shard_map/dot_general | solution.py:418
  80.2 0.0 copy-done.3
  80.2 0.6 copy.16
  80.8 0.0 copy-done.2
  80.8 0.6 copy.17
Async XLA Ops:
  74.2 2.5 %copy-start = (bf16[4,4,16,2304]{3,2,1,0:T(8,128)(2,1)S(1)}, bf16[4,4,16,2304]{3,2,1,0:T(8,128)(2,1)}, u32[]{:S(2)}) copy-start(bf16[4,4,16,2304]{3,2,1,0:T(8,128)(2,1)} %get-tuple-element.11) | copy-start | bytes 3538948
  74.2 4.7 %copy-start.1 = (bf16[4,64,1024]{2,1,0:T(8,128)(2,1)S(1)}, bf16[4,64,1024]{2,1,0:T(8,128)(2,1)}, u32[]{:S(2)}) copy-start(bf16[4,64,1024]{2,1,0:T(8,128)(2,1)} %get-tuple-element.12) | copy-start | bytes 1572868
  76.7 3.5 %copy-start.3 = (bf16[16,512]{1,0:T(8,128)(2,1)S(1)}, bf16[16,512]{1,0:T(8,128)(2,1)}, u32[]{:S(2)}) copy-start(bf16[16,512]{1,0:T(8,128)(2,1)} %get-tuple-element.18) | copy-start | bytes 49156
  76.7 4.1 %copy-start.2 = (bf16[16,512]{1,0:T(8,128)(2,1)S(1)}, bf16[16,512]{1,0:T(8,128)(2,1)}, u32[]{:S(2)}) copy-start(bf16[16,512]{1,0:T(8,128)(2,1)} %get-tuple-element.19) | copy-start | bytes 49156

commit v3 on v2

--- a/solution.py
+++ b/solution.py
@@ -38,15 +38,22 @@
 
 
 def routed(
-    ids_ref,
-    probs_ref,
-    tokens_ref,
-    cot_ref,
+    ids_hbm,
+    probs_hbm,
+    tokens_hbm,
+    cot_hbm,
     gate_hbm,
     up_hbm,
     down_hbm,
     mixed_ref,
     grad_ref,
+    grad_gate_ref,
+    grad_up_ref,
+    grad_down_ref,
+    ids_ref,
+    probs_ref,
+    tokens_ref,
+    cot_ref,
     xin,
     acts,
     gate_ref,
@@ -82,8 +89,11 @@
     sides = ((right, e), (left, e))
     near = (right, left)
 
+    turned = [yc] + [lax.rem(yc + i, 16) for i in range(1, 16)]
+    planes = [z * 16] + [lax.rem(z + d, 8) * 16 for d in range(1, 8)]
+
     def plane(d, row):
-        return (x, lax.rem(z + d, 8) * 16 + row)
+        return (x, planes[d % 8] + row)
 
     def greet(sem, device):
         pl.semaphore_signal(sem, inc=1, device_id=device, device_id_type=MESH)
@@ -100,25 +110,39 @@
         copy.start()
         return copy
 
+    loads = []
+    for i, (src, dst) in enumerate(
+        (
+            (ids_hbm, ids_ref),
+            (probs_hbm, probs_ref),
+            (tokens_hbm, tokens_ref),
+            (cot_hbm, cot_ref),
+            (gate_hbm.at[0], gate_ref),
+            (up_hbm.at[0], up_ref),
+            (down_hbm.at[0], down_ref),
+        )
+    ):
+        load = pltpu.make_async_copy(src, dst, load_sem.at[i])
+        load.start()
+        loads.append(load)
     barrier = pltpu.get_barrier_semaphore()
     for side in sides:
         greet(barrier, side)
     for d in range(1, 8):
         greet(barrier, plane(d, yc))
     for i in range(1, 16):
-        greet(barrier, plane(0, lax.rem(yc + i, 16)))
-    loads = []
-    for i, (src, dst) in enumerate(
-        ((gate_hbm, gate_ref), (up_hbm, up_ref), (down_hbm, down_ref))
-    ):
-        load = pltpu.make_async_copy(src.at[0], dst, load_sem.at[i])
-        load.start()
-        loads.append(load)
-
-    lane = iota((16, 128), 1)
-    own_token = iota((16, 128), 0) == lane % 16
-    ids = ids_ref[...].astype(F32)
-    probs = probs_ref[...]
+        greet(barrier, plane(0, turned[i]))
+    for load in loads[:4]:
+        load.wait()
+    own_token = (iota((16, 128), 0) == iota((16, 128), 1) % 16).astype(F32)
+
+    def replicate(rows):
+        return jnp.dot(
+            rows, own_token, precision=lax.Precision.HIGHEST, preferred_element_type=F32
+        )
+
+    ids = replicate(ids_ref[...].astype(F32))
+    probs = replicate(probs_ref[...])
     rows = iota((128, 128), 0)
     cols = iota((128, 128), 1)
     turn = rows // 16
@@ -127,13 +151,9 @@
     taken = jnp.zeros((128, 128), F32)
     weight = jnp.zeros((128, 128), F32)
     for k in range(8):
-        id_row = jnp.sum(jnp.where(own_token, ids[:, k : k + 1], 0.0), axis=0, keepdims=True)
-        prob_row = jnp.sum(
-            jnp.where(own_token, probs[:, k : k + 1], 0.0), axis=0, keepdims=True
-        )
-        same = expert == id_row
+        same = expert == ids[k : k + 1]
         taken = jnp.where(same, 1.0, taken)
-        weight = jnp.where(same, prob_row, weight)
+        weight = jnp.where(same, probs[k : k + 1], weight)
     earlier = ((rows // 16 == cols // 16) & (rows < cols)).astype(F32).astype(BF16)
     rank = dot(taken.astype(BF16), earlier)
     code = jnp.where(taken > 0.0, (cols // 16 * 2).astype(F32) + rank, -1.0)
@@ -157,7 +177,7 @@
         full = jnp.where(mine, value[:, None, :], 0.0)
         return full.reshape(256, 128)
 
-    for q in range(8):
+    def select(q):
         part_rows = slice(16 * q, 16 * (q + 1))
         mine = code[part_rows][:, None, :] == slot
         high = expand(out_high[part_rows], mine).astype(BF16)
@@ -165,14 +185,8 @@
         sent = dot(high, features) + dot(low, features)
         out_box[q] = sent.astype(BF16).reshape(16, 16, 128)
 
-    pl.semaphore_wait(barrier, 24)
-    for d in range(1, 8):
-        greet(ready, plane(d, yc))
-    keep = pltpu.make_async_copy(out_box.at[0, yc], in_box.at[0, yc], local_sem.at[0])
-    keep.start()
-
     def send_to(q, i):
-        row = lax.rem(yc + i, 16)
+        row = turned[i]
         k, j = q // (8 // CHUNKS), q % (8 // CHUNKS)
         push(
             out_box.at[q, row],
@@ -183,15 +197,22 @@
         )
 
     def send_group(q, first):
-        def body(i, carry):
+        for i in range(first, 16):
             send_to(q, i)
-            return carry
-
-        lax.fori_loop(first, 16, body, 0)
+
+    select(0)
+    pl.semaphore_wait(barrier, 24)
+    for d in range(1, 8):
+        greet(ready, plane(d, yc))
+    keep = pltpu.make_async_copy(out_box.at[0, yc], in_box.at[0, yc], local_sem.at[0])
+    keep.start()
 
     send_group(0, 1)
+    select(1)
     pl.semaphore_wait(ready, 7)
-    for q in range(1, 8):
+    send_group(1, 0)
+    for q in range(2, 8):
+        select(q)
         send_group(q, 0)
 
     for q in range(8):
@@ -212,7 +233,7 @@
         & (big_col % 32 // 2 == big_row // 16)
         & (big_row % 2 == big_col % 2)
     ).astype(F32).astype(BF16)
-    for load in loads:
+    for load in loads[4:]:
         load.wait()
     keep.wait()
 
@@ -312,18 +333,14 @@
         for j in range(8 // CHUNKS):
             q = k * (8 // CHUNKS) + j
 
-            def body(i, carry, j=j, q=q):
-                row = lax.rem(yc + i, 16)
+            for i in range(1 if q == 0 else 0, 16):
                 push(
-                    home_box.at[k, j * 16 + row],
+                    home_box.at[k, j * 16 + turned[i]],
                     back_box.at[k, j * 16 + yc],
                     home_send,
                     home_recv.at[k],
-                    plane(8 - ORDER[q], row),
+                    plane(8 - ORDER[q], turned[i]),
                 )
-                return carry
-
-            lax.fori_loop(1 if q == 0 else 0, 16, body, 0)
         if k == 0:
             copy = pltpu.make_async_copy(
                 home_box.at[0, yc], back_box.at[0, yc], local_sem.at[1]
@@ -336,6 +353,18 @@
         for s in reversed(range(len(stages))):
             if 0 <= t - s < CHUNKS:
                 stages[s](t - s)
+
+    h_all = acts[...].reshape(256, WIDE)
+    x_all = xin[...].reshape(256, 2 * COLUMNS)
+
+    def outer(a, b):
+        return lax.dot_general(
+            a, b, (((0,), (0,)), ((), ())), preferred_element_type=F32
+        ).astype(BF16)
+
+    grad_gate_ref[...] = outer(h_all[:, FF : 2 * FF], x_all[:, :COLUMNS])
+    grad_up_ref[...] = outer(h_all[:, 2 * FF :], x_all[:, :COLUMNS])
+    grad_down_ref[...] = outer(h_all[:, :FF], x_all[:, COLUMNS:])
 
     total = jnp.zeros((128, 128), F32)
     for k in range(CHUNKS):
@@ -362,25 +391,45 @@
     wait_bytes(back_box.at[0, pl.ds(0, SOURCES - 1)], home_send)
 
 
+def store(*refs):
+    sources, targets, sems = refs[:5], refs[5:10], refs[10]
+    copies = [
+        pltpu.make_async_copy(src, dst, sems.at[i])
+        for i, (src, dst) in enumerate(zip(sources, targets))
+    ]
+    for copy in copies:
+        copy.start()
+    for copy in copies:
+        copy.wait()
+
+
 def on_device(tokens, cotangent, expert_ids, gate_probs, w_gate, w_up, w_down):
     vmem = pl.BlockSpec(memory_space=pltpu.VMEM)
     hbm = pl.BlockSpec(memory_space=pl.ANY)
+    far = pl.BlockSpec(memory_space=pltpu.MemorySpace.HBM)
 
     def buf(*shape):
         return pltpu.VMEM(shape, BF16)
 
     dma = pltpu.SemaphoreType.DMA
-    mixed, grad_tokens, xin, acts = pl.pallas_call(
+    results = pl.pallas_call(
         routed,
         out_shape=(
             jax.ShapeDtypeStruct((16, COLUMNS), BF16),
             jax.ShapeDtypeStruct((16, COLUMNS), BF16),
-            jax.ShapeDtypeStruct((CHUNKS, ROWS, 2 * COLUMNS), BF16),
-            jax.ShapeDtypeStruct((CHUNKS, 4, PIECE, WIDE), BF16),
+            jax.ShapeDtypeStruct((FF, COLUMNS), BF16),
+            jax.ShapeDtypeStruct((FF, COLUMNS), BF16),
+            jax.ShapeDtypeStruct((FF, COLUMNS), BF16),
         ),
-        in_specs=[vmem] * 4 + [hbm] * 3,
-        out_specs=(vmem, vmem, vmem, vmem),
+        in_specs=[far] * 7,
+        out_specs=(vmem,) * 5,
         scratch_shapes=[
+            pltpu.VMEM((8, 16), jnp.int32),
+            pltpu.VMEM((8, 16), F32),
+            buf(16, COLUMNS),
+            buf(16, COLUMNS),
+            buf(CHUNKS, ROWS, 2 * COLUMNS),
+            buf(CHUNKS, 4, PIECE, WIDE),
             buf(FF, COLUMNS),
             buf(FF, COLUMNS),
             buf(FF, COLUMNS),
@@ -396,7 +445,7 @@
             buf(CHUNKS, PIECE, WIDE),
             buf(CHUNKS, 2, PIECE, WIDE),
             buf(CHUNKS, 2, PIECE, WIDE),
-            dma((3,)),
+            dma((7,)),
             dma((2,)),
             dma,
             dma((CHUNKS,)),
@@ -407,20 +456,19 @@
             pltpu.SemaphoreType.REGULAR,
         ],
         compiler_params=pltpu.CompilerParams(
-            collective_id=0, has_side_effects=True, vmem_limit_bytes=60 * 1024 * 1024
+            collective_id=0, has_side_effects=True, vmem_limit_bytes=51 * 1024 * 1024
         ),
-    )(expert_ids, gate_probs, tokens, cotangent, w_gate, w_up, w_down)
-    x_in = xin.reshape(256, 2 * COLUMNS)
-    h = acts.reshape(256, WIDE)
-    over_rows = (((0,), (0,)), ((), ()))
-
-    def outer(a, b):
-        return lax.dot_general(a, b, over_rows, preferred_element_type=F32).astype(BF16)[None]
-
-    grad_gate = outer(h[:, FF : 2 * FF], x_in[:, :COLUMNS])
-    grad_up = outer(h[:, 2 * FF :], x_in[:, :COLUMNS])
-    grad_down = outer(h[:, :FF], x_in[:, COLUMNS:])
-    return (mixed, grad_tokens, grad_gate, grad_up, grad_down)
+    )(*[pltpu.with_memory_space_constraint(a, pltpu.MemorySpace.HBM) for a in (expert_ids.T, gate_probs.T, tokens, cotangent, w_gate, w_up, w_down)])
+    shapes = [jax.ShapeDtypeStruct(r.shape, r.dtype) for r in results]
+    mixed, grad_tokens, grad_gate, grad_up, grad_down = pl.pallas_call(
+        store,
+        out_shape=shapes,
+        in_specs=[vmem] * 5,
+        out_specs=[hbm] * 5,
+        scratch_shapes=[dma((5,))],
+        compiler_params=pltpu.CompilerParams(vmem_limit_bytes=4 * 1024 * 1024),
+    )(*results)
+    return (mixed, grad_tokens, grad_gate[None], grad_up[None], grad_down[None])
 
 
 def solution(mesh):

time: 81.8 us -> 71.5 us (0.87)
  matrix products: 5.98 us -> 0 us
  local copies, waits for them, and re-layouts: 3.94 us -> 0 us
    dot_general x3 -> x0, matrix products: 5.98 us -> none  [outer(): lax.dot_general(a, b, over_rows, preferred_element_type=F32).astype(BF16)]
    unnamed x12 -> x0, local copies, waits for them, and re-layouts: 3.94 us -> none
    pallas_call x1, Pallas kernels: 70.9 us -> 69.3 us  [on_device(): pl.pallas_call(routed, out_shape=(jax.ShapeDtypeStruct((16, COLUMNS), BF1...]
    pallas_call x0 -> x1, Pallas kernels: none -> 1.46 us  [on_device(): pl.pallas_call(store, out_shape=shapes, in_specs=[vmem] * 5, out_specs=[h...]
where the time goes in v3:
time: 71.5 us; the launch traced here: 71.4 us
  Pallas kernels  70.8 us (99%)
    pallas_call x1, Pallas kernels, on_device(): pl.pallas_call(routed, out_shape=(jax.ShapeDtypeStruct((16, COLUMNS), BF1...  69.3 us
    pallas_call x1, Pallas kernels, on_device(): pl.pallas_call(store, out_shape=shapes, in_specs=[vmem] * 5, out_specs=[h...  1.46 us

profile of v3, /device:TPU:1, one launch (start us, length us, event | category | flops | bytes accessed | tf_op | source)
XLA Modules:
  0.0 71.4 jit_solution(18422114731703248133)
XLA Ops:
  0.6 69.3 %shard_map.110 = (bf16[16,512]{1,0:T(8,128)(2,1)S(1)}, bf16[16,512]{1,0:T(8,128)(2,1)S(1)}, bf16[768,512]{1,0:T(8,128)(2,1)S(1)}, bf16[768,512]{1,0:T(8,128)(2,1)S(1)}, bf16[768,512]{1,0:T(8,128)(2,1)S(1)}) custom-call(s32[8,16]{1,0:T(8,128)} %bitcast.5, f32[8,16]{1,0:T(8,128)} %bitcast.6, bf16[16,512]{1,0:T(8,128)(2,1)} %tokens_hbm.1, ...), custom_call_target="tpu_custom_call" | custom-call | tf_op jit(solution)/shard_map/pallas_call | solution.py:415
  70.0 1.5 %shard_map.111 = (bf16[16,512]{1,0:T(8,128)(2,1)}, bf16[16,512]{1,0:T(8,128)(2,1)}, bf16[768,512]{1,0:T(8,128)(2,1)}, bf16[768,512]{1,0:T(8,128)(2,1)}, bf16[768,512]{1,0:T(8,128)(2,1)}) custom-call(bf16[16,512]{1,0:T(8,128)(2,1)S(1)} %get-tuple-element.15.refs_0_, bf16[16,512]{1,0:T(8,128)(2,1)S(1)} %get-tuple-element.16.refs_1_, ...), custom_call_target="tpu_custom_call" | custom-call | tf_op jit(solution)/shard_map/pallas_call | solution.py:463

commit v4 on v3

--- a/solution.py
+++ b/solution.py
@@ -203,16 +203,14 @@
     select(0)
     pl.semaphore_wait(barrier, 24)
     for d in range(1, 8):
-        greet(ready, plane(d, yc))
+        greet(ready.at[8 - d], plane(d, yc))
     keep = pltpu.make_async_copy(out_box.at[0, yc], in_box.at[0, yc], local_sem.at[0])
     keep.start()
 
     send_group(0, 1)
-    select(1)
-    pl.semaphore_wait(ready, 7)
-    send_group(1, 0)
-    for q in range(2, 8):
+    for q in range(1, 8):
         select(q)
+        pl.semaphore_wait(ready.at[ORDER[q]], 1)
         send_group(q, 0)
 
     for q in range(8):
@@ -350,7 +348,7 @@
 
     stages = (stage_partial, stage_sum, stage_act, stage_forward, stage_home)
     for t in range(CHUNKS + len(stages) - 1):
-        for s in reversed(range(len(stages))):
+        for s in range(len(stages)):
             if 0 <= t - s < CHUNKS:
                 stages[s](t - s)
 
@@ -453,7 +451,7 @@
             dma((CHUNKS,)),
             dma((4, CHUNKS, 2)),
             dma((4, CHUNKS, 2)),
-            pltpu.SemaphoreType.REGULAR,
+            pltpu.SemaphoreType.REGULAR((8,)),
         ],
         compiler_params=pltpu.CompilerParams(
             collective_id=0, has_side_effects=True, vmem_limit_bytes=51 * 1024 * 1024

time: 71.5 us -> 66.6 us (0.931)
  Pallas kernels: 70.8 us -> 65.8 us
    pallas_call x1, Pallas kernels: 69.3 us -> 64.4 us  [on_device(): pl.pallas_call(routed, out_shape=(jax.ShapeDtypeStruct((16, COLUMNS), BF1...]
where the time goes in v4:
time: 66.6 us; the launch traced here: 66.5 us
  Pallas kernels  65.8 us (99%)
    pallas_call x1, Pallas kernels, on_device(): pl.pallas_call(routed, out_shape=(jax.ShapeDtypeStruct((16, COLUMNS), BF1...  64.4 us
    pallas_call x1, Pallas kernels, on_device(): pl.pallas_call(store, out_shape=shapes, in_specs=[vmem] * 5, out_specs=[h...  1.46 us

profile of v4, /device:TPU:1, one launch (start us, length us, event | category | flops | bytes accessed | tf_op | source)
XLA Modules:
  0.0 66.5 jit_solution(13238103461980108481)
XLA Ops:
  0.6 64.4 %shard_map.110 = (bf16[16,512]{1,0:T(8,128)(2,1)S(1)}, bf16[16,512]{1,0:T(8,128)(2,1)S(1)}, bf16[768,512]{1,0:T(8,128)(2,1)S(1)}, bf16[768,512]{1,0:T(8,128)(2,1)S(1)}, bf16[768,512]{1,0:T(8,128)(2,1)S(1)}) custom-call(s32[8,16]{1,0:T(8,128)} %bitcast.5, f32[8,16]{1,0:T(8,128)} %bitcast.6, bf16[16,512]{1,0:T(8,128)(2,1)} %tokens_hbm.1, ...), custom_call_target="tpu_custom_call" | custom-call | tf_op jit(solution)/shard_map/pallas_call | solution.py:413
  65.0 1.5 %shard_map.111 = (bf16[16,512]{1,0:T(8,128)(2,1)}, bf16[16,512]{1,0:T(8,128)(2,1)}, bf16[768,512]{1,0:T(8,128)(2,1)}, bf16[768,512]{1,0:T(8,128)(2,1)}, bf16[768,512]{1,0:T(8,128)(2,1)}) custom-call(bf16[16,512]{1,0:T(8,128)(2,1)S(1)} %get-tuple-element.15.refs_0_, bf16[16,512]{1,0:T(8,128)(2,1)S(1)} %get-tuple-element.16.refs_1_, ...), custom_call_target="tpu_custom_call" | custom-call | tf_op jit(solution)/shard_map/pallas_call | solution.py:461

commit v5 on v4

--- a/solution.py
+++ b/solution.py
@@ -213,13 +213,14 @@
         pl.semaphore_wait(ready.at[ORDER[q]], 1)
         send_group(q, 0)
 
-    for q in range(8):
+    def weigh(q):
         part_rows = slice(16 * q, 16 * (q + 1))
         mine = code[part_rows][:, None, :] == slot
         high = expand(back_high[part_rows], mine)
         low = expand(back_low[part_rows], mine)
         back_hi[:, q * 256 : (q + 1) * 256] = high.T.astype(BF16)
         back_lo[:, q * 256 : (q + 1) * 256] = low.T.astype(BF16)
+
     big_row, big_col = iota((256, 256), 0), iota((256, 256), 1)
     gather[...] = (
         (big_row // 32 == big_col % 16 // 2)
@@ -266,22 +267,24 @@
             part[k, :, :, n * FF : (n + 1) * FF] = value.reshape(4, PIECE, FF)
         for i in range(2):
             hop(0, k, i, part.at[k, opposite, :, halves(i)], first_in.at[k, :, halves(i)])
+        for i in range(2):
+            other = halves(1 - i)
+            hop(4, k, i, part.at[k, near[i], :, other], second_in.at[k, i, :, other])
 
     def stage_sum(k):
         for i in range(2):
             ring[0, k, i].wait_recv()
         for i in range(2):
             span = slice(HALF * i, HALF * (i + 1))
-            rest = slice(HALF * (1 - i), HALF * (2 - i))
-            second_out[k, i, :, span] = (
+            second_out[k, i] = (
                 part[k, near[i], :, span].astype(F32) + first_in[k, :, span].astype(F32)
             ).astype(BF16)
-            second_out[k, i, :, rest] = part[k, near[i], :, rest]
-        for i in range(2):
-            hop(1, k, i, second_out.at[k, i], second_in.at[k, i])
+        for i in range(2):
+            hop(1, k, i, second_out.at[k, i], second_in.at[k, i, :, halves(i)])
 
     def stage_act(k):
         for i in range(2):
+            ring[4, k, i].wait_recv()
             ring[1, k, i].wait_recv()
 
         def total(n):
@@ -351,6 +354,9 @@
         for s in range(len(stages)):
             if 0 <= t - s < CHUNKS:
                 stages[s](t - s)
+        if 1 <= t <= 4:
+            weigh(2 * t - 2)
+            weigh(2 * t - 1)
 
     h_all = acts[...].reshape(256, WIDE)
     x_all = xin[...].reshape(256, 2 * COLUMNS)
@@ -379,7 +385,7 @@
         mixed_ref[:, g * 128 : (g + 1) * 128] = result[16 * g : 16 * (g + 1)]
         grad_ref[:, g * 128 : (g + 1) * 128] = result[64 + 16 * g : 64 + 16 * (g + 1)]
 
-    for stage in range(4):
+    for stage in range(5):
         for k in range(CHUNKS):
             for i in range(2):
                 ring[stage, k, i].wait_send()
@@ -441,7 +447,7 @@
             buf(256, 256),
             buf(CHUNKS, 4, PIECE, WIDE),
             buf(CHUNKS, PIECE, WIDE),
-            buf(CHUNKS, 2, PIECE, WIDE),
+            buf(CHUNKS, 2, PIECE, HALF),
             buf(CHUNKS, 2, PIECE, WIDE),
             dma((7,)),
             dma((2,)),
@@ -449,8 +455,8 @@
             dma((CHUNKS,)),
             dma,
             dma((CHUNKS,)),
-            dma((4, CHUNKS, 2)),
-            dma((4, CHUNKS, 2)),
+            dma((5, CHUNKS, 2)),
+            dma((5, CHUNKS, 2)),
             pltpu.SemaphoreType.REGULAR((8,)),
         ],
         compiler_params=pltpu.CompilerParams(

time: 66.6 us -> 66 us (level)
  no operation moved by 1% of the time
where the time goes in v5:
time: 66 us; the launch traced here: 65.9 us
  Pallas kernels  65.2 us (99%)
    pallas_call x1, Pallas kernels, on_device(): pl.pallas_call(routed, out_shape=(jax.ShapeDtypeStruct((16, COLUMNS), BF1...  63.8 us
    pallas_call x1, Pallas kernels, on_device(): pl.pallas_call(store, out_shape=shapes, in_specs=[vmem] * 5, out_specs=[h...  1.46 us

profile of v5, /device:TPU:1, one launch (start us, length us, event | category | flops | bytes accessed | tf_op | source)
XLA Modules:
  0.0 65.9 jit_solution(4548290487390921667)
XLA Ops:
  0.6 63.8 %shard_map.110 = (bf16[16,512]{1,0:T(8,128)(2,1)S(1)}, bf16[16,512]{1,0:T(8,128)(2,1)S(1)}, bf16[768,512]{1,0:T(8,128)(2,1)S(1)}, bf16[768,512]{1,0:T(8,128)(2,1)S(1)}, bf16[768,512]{1,0:T(8,128)(2,1)S(1)}) custom-call(s32[8,16]{1,0:T(8,128)} %bitcast.5, f32[8,16]{1,0:T(8,128)} %bitcast.6, bf16[16,512]{1,0:T(8,128)(2,1)} %tokens_hbm.1, ...), custom_call_target="tpu_custom_call" | custom-call | tf_op jit(solution)/shard_map/pallas_call | solution.py:419
  64.4 1.5 %shard_map.111 = (bf16[16,512]{1,0:T(8,128)(2,1)}, bf16[16,512]{1,0:T(8,128)(2,1)}, bf16[768,512]{1,0:T(8,128)(2,1)}, bf16[768,512]{1,0:T(8,128)(2,1)}, bf16[768,512]{1,0:T(8,128)(2,1)}) custom-call(bf16[16,512]{1,0:T(8,128)(2,1)S(1)} %get-tuple-element.15.refs_0_, bf16[16,512]{1,0:T(8,128)(2,1)S(1)} %get-tuple-element.16.refs_1_, ...), custom_call_target="tpu_custom_call" | custom-call | tf_op jit(solution)/shard_map/pallas_call | solution.py:467
